TPU v7x, 256 devices: a whole 4x4x8 slice. The times are simulated.
256 devices in a mesh: camframe: 64 (over z_hi, y, x), row: 4 (over z_lo, core).
Axes of the slice: x: 4, y: 4, z: 8 (z_hi: 4, z_lo: 2; z = z_hi * 2 + z_lo), core: 2. Of those that a mesh axis runs over, the one named last changes fastest.
Arguments:
- tokens: bfloat16 [192, 12, 48, 1152], P('camframe', 'row'), may hold values from -40 to 40
- classes: int32 [192, 12, 48], P('camframe', 'row'), may hold values from 0 to 7
- tile_lists: int32 [192, 12, 3, 8], P('camframe', 'row'), may hold values from -1 to 11, as said below
- kv_cache: bfloat16 [192, 12, 2, 8, 2304], P('camframe', 'row'), may hold values from -200 to 200
- camera_loop: int32 [6, 2], replicated, may hold values from 0 to 5, as said below
- class_weight: bfloat16 [72, 1152], replicated, may hold values from -2 to 2
- depth_weight: bfloat16 [9, 1152], replicated, may hold values from -2 to 2
- zero_weight: bfloat16 [1152, 1152], replicated, may hold values from -0.1875 to 0.1875
- norm_gain: float32 [1152], replicated, may hold values from 0.25 to 1.75
- query_weight: bfloat16 [1152, 1152], replicated, may hold values from -0.1875 to 0.1875
- out_weight: bfloat16 [1152, 1152], replicated, may hold values from -0.1875 to 0.1875
Outputs:
- result: bfloat16 [192, 12, 48, 1152], P('camframe', 'row')
Inputs may be any that keep to these rules, and one draw needn't show every extreme that they name: `tile_lists`: slot 0 of every list holds an entry below 6; the entries of one list that are not -1 are distinct. camera_loop[c, 0] and camera_loop[c, 1] are the cameras before and after camera c on one cycle through all 6 cameras.
All inputs are finite; a program needn't handle non-finite values.
Results may differ from a plain program's by a relative error of at most 0.0072.
Values may be sent and summed in bfloat16 or wider, within the bound.
No kernel may reach another device: no remote copies, remote signals or barrier semaphores. Data moves between devices by JAX's collectives and lax.ppermute only.
A program may use at most 128 MiB of HBM per device.

v0:
```python
import jax
import jax.numpy as jnp
from jax import lax
from jax.sharding import PartitionSpec as P

HEADS = 16
HEAD = 72
CAMS = 6
CLASSES = 8
QT = 16


def with_halo(cells, sides, width):
    for axis, dim in sides:
        count = lax.axis_size(axis)
        ends = count - 1
        head = lax.slice_in_dim(cells, 0, width, axis=dim)
        tail = lax.slice_in_dim(cells, cells.shape[dim] - width, cells.shape[dim], axis=dim)
        cells = jnp.concatenate(
            [
                lax.ppermute(tail, axis, [(i, (i + 1) % count) for i in range(ends)]),
                cells,
                lax.ppermute(head, axis, [((i + 1) % count, i) for i in range(ends)]),
            ],
            axis=dim,
        )
    return cells


def passed_along(block, axis, distance):
    devices = range(lax.axis_size(axis))
    route = [(i - distance, i) for i in devices if i - distance in devices]
    return lax.ppermute(block, axis, route)


def one_hot_conv(class_ext, row_start, total_rows, class_weight):
    view_count, ext_rows, col_count = class_ext.shape
    global_row = row_start + jnp.arange(ext_rows, dtype=jnp.int32)
    inside = (global_row >= 0) & (global_row < total_rows)
    onehot = (
        (class_ext[..., None] == jnp.arange(CLASSES, dtype=jnp.int32)) & inside[None, :, None, None]
    ).astype(jnp.bfloat16)
    padded = jnp.pad(onehot, ((0, 0), (0, 0), (1, 1), (0, 0)))
    out_rows = ext_rows - 2
    stacked = jnp.concatenate(
        [
            padded[:, row_tap : row_tap + out_rows, col_tap : col_tap + col_count]
            for row_tap in range(3)
            for col_tap in range(3)
        ],
        axis=-1,
    )
    flat_taps = stacked.reshape(view_count * out_rows * col_count, 9 * CLASSES)
    feature = jax.nn.silu(jnp.dot(flat_taps, class_weight, preferred_element_type=jnp.float32))
    return feature.astype(jnp.bfloat16).reshape(
        view_count, out_rows, col_count, class_weight.shape[1]
    )


def body(
    tokens,
    classes,
    tile_lists,
    kv_cache,
    camera_loop,
    class_weight,
    depth_weight,
    zero_weight,
    norm_gain,
    query_weight,
    out_weight,
):
    view_count, rows_dev, col_count, d_model = tokens.shape
    edge_cols = kv_cache.shape[3]
    slot_count = tile_lists.shape[3]
    row_start = lax.axis_index("row") * rows_dev
    total_rows = rows_dev * lax.axis_size("row")
    class_ext = with_halo(classes, (("row", 1),), 1)
    feature = one_hot_conv(class_ext, row_start - 1, total_rows, class_weight)
    feature_ext = with_halo(feature, (("row", 1),), 1)
    feat_pad = jnp.pad(feature_ext, ((0, 0), (0, 0), (1, 1), (0, 0)))
    depthwise = jnp.zeros((view_count, rows_dev, col_count, d_model), jnp.float32)
    for row_tap in range(3):
        for col_tap in range(3):
            depthwise = (
                depthwise
                + depth_weight[3 * row_tap + col_tap].astype(jnp.float32)
                * feat_pad[:, row_tap : row_tap + rows_dev, col_tap : col_tap + col_count]
            )
    depthwise = depthwise.astype(jnp.bfloat16).reshape(-1, d_model)
    hidden = tokens.reshape(-1, d_model).astype(jnp.float32) + jnp.dot(
        depthwise, zero_weight, preferred_element_type=jnp.float32
    )
    normed = (
        hidden * lax.rsqrt(jnp.mean(hidden * hidden, axis=-1, keepdims=True) + 1e-06) * norm_gain
    ).astype(jnp.bfloat16)
    queries = jnp.dot(normed, query_weight, preferred_element_type=jnp.float32).astype(jnp.bfloat16)
    position = lax.axis_index("camframe")
    frame_idx = position // 2
    frame_half = position % 2
    is_lower = frame_half == 0
    nearby = {}
    for offset in (1, -1):
        nearby[offset] = passed_along(kv_cache, "camframe", offset)
    lower = jnp.where(is_lower, kv_cache, nearby[1])
    upper = jnp.where(is_lower, nearby[-1], kv_cache)
    earlier = {}
    for offset in (2, 3):
        earlier[offset] = passed_along(kv_cache, "camframe", offset)
    prev_lower = jnp.where(is_lower, earlier[2], earlier[3])
    prev_upper = jnp.where(is_lower, nearby[1], earlier[2])
    candidates = jnp.stack([jnp.stack([lower, upper]), jnp.stack([prev_lower, prev_upper])])
    cache_flat = candidates.reshape(-1, 2 * d_model)
    cameras = frame_half * view_count + jnp.arange(view_count, dtype=jnp.int32)
    camera_pick = (jnp.arange(CAMS, dtype=jnp.int32)[None, :] == cameras[:, None]).astype(jnp.int32)
    loop_rows = jnp.sum(camera_pick[:, :, None] * camera_loop[None], axis=1)
    clipped = jnp.maximum(tile_lists, 0)
    step_back = clipped // (2 * rows_dev)
    side_pick = clipped // rows_dev % 2
    key_row = clipped % rows_dev
    live_slot = (tile_lists >= 0) & (frame_idx >= step_back)
    neighbour = jnp.where(
        side_pick == 0, loop_rows[:, 0][:, None, None, None], loop_rows[:, 1][:, None, None, None]
    )
    tile_id = ((step_back * CAMS + neighbour) * rows_dev + key_row) * 2 + (1 - side_pick)
    tile_count = 2 * CAMS * rows_dev * 2
    tile_per_row = col_count // QT
    score_scale = HEAD ** (-0.5)
    tile_groups = view_count * rows_dev * tile_per_row
    tile_table = cache_flat.reshape(tile_count, edge_cols, 2 * d_model)
    slot_tiles = jnp.take(tile_table, tile_id.reshape(-1), axis=0)
    slot_tiles = slot_tiles.reshape(tile_groups, slot_count * edge_cols, 2 * d_model)
    slot_keys = slot_tiles[..., :d_model].reshape(tile_groups, slot_count * edge_cols, HEADS, HEAD)
    slot_values = slot_tiles[..., d_model:].reshape(
        tile_groups, slot_count * edge_cols, HEADS, HEAD
    )
    query_tiles = queries.reshape(tile_groups, QT, HEADS, HEAD)
    scores = (
        jnp.einsum("nthd,nkhd->nhtk", query_tiles, slot_keys, preferred_element_type=jnp.float32)
        * score_scale
    )
    slot_mask = jnp.repeat(live_slot.reshape(tile_groups, slot_count), edge_cols, axis=-1)[
        :, None, None, :
    ]
    scores = jnp.where(slot_mask, scores, -1e30)
    row_max = jnp.max(scores, axis=-1, keepdims=True)
    exponent = jnp.exp(scores - row_max)
    weights_bf = (exponent / jnp.sum(exponent, axis=-1, keepdims=True)).astype(jnp.bfloat16)
    attended = jnp.einsum(
        "nhtk,nkhd->nthd", weights_bf, slot_values, preferred_element_type=jnp.float32
    ).astype(jnp.bfloat16)
    attended = attended.reshape(-1, d_model)
    result = hidden + jnp.dot(attended, out_weight, preferred_element_type=jnp.float32)
    return result.astype(jnp.bfloat16).reshape(view_count, rows_dev, col_count, d_model)


def solution(mesh):
    return jax.shard_map(
        body,
        mesh=mesh,
        in_specs=(
            P("camframe", "row", None, None),
            P("camframe", "row", None),
            P("camframe", "row", None, None),
            P("camframe", "row", None, None, None),
            P(),
            P(),
            P(),
            P(),
            P(),
            P(),
            P(),
        ),
        out_specs=P("camframe", "row", None, None),
        check_vma=False,
    )
```

profile of v0, /device:TPU:101, one launch (start us, length us, event | category | flops | bytes accessed | tf_op | source)
XLA Modules:
  0.0 180.5 jit_solution(945304682349822389)
XLA Ops:
  0.0 0.0 copy-start
  0.0 3.1 %collective-permute-start.4 = (bf16[3,3,2,8,2304]{4,3,2,1,0:T(8,128)(2,1)}, bf16[3,3,2,8,2304]{4,3,2,1,0:T(8,128)(2,1)}, u32[]{:S(2)}, u32[]{:S(2)}) collective-permute-start(bf16[3,3,2,8,2304]{4,3,2,1,0:T(8,128)(2,1)} %param.14), channel_id=1, source_target_pairs={{0,4},{4,8},{8,12},{12,16},{16,20},{20,24},{24,28},{28,32},{32,36}... | collective-permute-start | bytes 1990664 | tf_op jit(solution)/shard_map/ppermute | solution.py:33
  3.1 2.5 %collective-permute-start.5 = (bf16[3,3,2,8,2304]{4,3,2,1,0:T(8,128)(2,1)}, bf16[3,3,2,8,2304]{4,3,2,1,0:T(8,128)(2,1)}, u32[]{:S(2)}, u32[]{:S(2)}) collective-permute-start(bf16[3,3,2,8,2304]{4,3,2,1,0:T(8,128)(2,1)} %param.14), channel_id=1, source_target_pairs={{4,0},{8,4},{12,8},{16,12},{20,16},{24,20},{28,24},{32,28},{36,32}... | collective-permute-start | bytes 1990664 | tf_op jit(solution)/shard_map/ppermute | solution.py:33
  5.6 5.3 %collective-permute-start.6 = (bf16[3,3,2,8,2304]{4,3,2,1,0:T(8,128)(2,1)}, bf16[3,3,2,8,2304]{4,3,2,1,0:T(8,128)(2,1)}, u32[]{:S(2)}, u32[]{:S(2)}) collective-permute-start(bf16[3,3,2,8,2304]{4,3,2,1,0:T(8,128)(2,1)} %param.14), channel_id=1, source_target_pairs={{0,8},{4,12},{8,16},{12,20},{16,24},{20,28},{24,32},{28,36},{32,40... | collective-permute-start | bytes 1990664 | tf_op jit(solution)/shard_map/ppermute | solution.py:33
  10.8 0.8 fusion.34
  11.6 1.3 collective-permute-start
  12.9 4.0 %collective-permute-start.1 = (s32[3,1,48]{2,1,0:T(1,128)S(1)}, s32[3,1,48]{2,1,0:T(1,128)S(1)}, u32[]{:S(2)}, u32[]{:S(2)}) collective-permute-start(s32[3,1,48]{2,1,0:T(1,128)S(1)} %get-tuple-element.34), channel_id=1, source_target_pairs={{1,0},{2,1},{3,2},{5,4},{6,5},{7,6},{9,8},{10,9},{11,10},{13,12},{... | collective-permute-start | bytes 1736 | tf_op jit(solution)/shard_map/ppermute | solution.py:23
  17.0 0.1 fusion.29
  17.0 0.8 multiply_reduce_fusion.1
  17.9 0.2 slice_reduce_fusion.1
  18.1 0.8 fusion.27
  18.9 0.1 copy.31
  19.0 0.8 compare_and_fusion
  19.8 0.1 copy.33
  19.9 0.6 reshape.190
  20.5 0.0 collective-permute-done
  20.5 0.0 collective-permute-done.1
  20.5 0.7 pad_add_fusion
  21.2 0.2 fusion.23
  21.4 0.8 pad_slice_fusion
  22.2 1.8 %concatenate.16 = bf16[3,3,48,72]{3,2,1,0:T(8,128)(2,1)} concatenate(bf16[3,3,48,8]{3,2,1,0:T(8,128)(2,1)} %get-tuple-element.32, bf16[3,3,48,8]{3,2,1,0:T(8,128)(2,1)S(1)} %get-tuple-element.31, bf16[3,3,48,8]{3,2,1,0:T(8,128)(2,1)S(1)} %get-tuple-element.25, bf16[3,3,48,8]{3,2,1,0:T(8,128)(2,1)S(1)} %get-tuple-element.26, bf16[3,3,48,8]{3,2,1,0:T(8,128)(2,1)S(1)} %get-tuple-element.30, ...), dimensions={3} | concatenate | bytes 124416 | tf_op jit(solution)/shard_map/concatenate | solution.py:45
  24.1 1.7 multiply_convert_fusion.1
  25.8 0.0 copy-start.4
  25.8 0.9 copy-done.4
  26.7 0.9 fusion.33
  27.6 1.3 collective-permute-start.2
  28.9 4.3 %collective-permute-start.3 = (bf16[3,1,48,1152]{3,2,1,0:T(8,128)(2,1)}, bf16[3,1,48,1152]{3,2,1,0:T(8,128)(2,1)S(1)}, u32[]{:S(2)}, u32[]{:S(2)}) collective-permute-start(bf16[3,1,48,1152]{3,2,1,0:T(8,128)(2,1)} %get-tuple-element.19), channel_id=1, source_target_pairs={{1,0},{2,1},{3,2},{5,4},{6,5},{7,6},{9,8},{10,9},{11,10},{13,12},{... | collective-permute-start | bytes 995336 | tf_op jit(solution)/shard_map/ppermute | solution.py:23
  33.2 0.1 copy.32
  33.3 0.1 copy.34
  33.4 0.0 copy-start.5
  33.4 0.0 copy-done.7
  33.5 0.1 convert_reduce_fusion.8
  33.6 0.0 collective-permute-done.2
  33.6 2.2 %collective-permute-start.7 = (bf16[3,3,2,8,2304]{4,3,2,1,0:T(8,128)(2,1)}, bf16[3,3,2,8,2304]{4,3,2,1,0:T(8,128)(2,1)}, u32[]{:S(2)}, u32[]{:S(2)}) collective-permute-start(bf16[3,3,2,8,2304]{4,3,2,1,0:T(8,128)(2,1)} %param.14), channel_id=1, source_target_pairs={{0,12},{4,16},{8,20},{12,24},{16,28},{20,32},{24,36},{28,40},{32,4... | collective-permute-start | bytes 1990664 | tf_op jit(solution)/shard_map/ppermute | solution.py:33
  35.8 0.0 collective-permute-done.3
  35.8 1.8 %fusion.12 = bf16[3,5,50,1152]{3,2,1,0:T(8,128)(2,1)S(1)} fusion(bf16[3,1,48,1152]{3,2,1,0:T(8,128)(2,1)S(1)} %collective-permute-done.3, bf16[3,3,48,1152]{3,2,1,0:T(8,128)(2,1)} %bitcast.41, bf16[3,1,48,1152]{3,2,1,0:T(8,128)(2,1)S(1)} %collective-permute-done.2), kind=kLoop, calls=%fused_computation.27 | loop fusion | flops 10368000 | bytes 3386880 | tf_op jit(solution)/shard_map/concatenate | solution.py:19
  37.7 0.0 copy-start.10
  37.7 2.1 %add_convert_fusion = bf16[3,3,48,1152]{3,2,1,0:T(8,128)(2,1)S(1)} fusion(bf16[3,3,48,1152]{3,2,1,0:T(8,128)(2,1)S(1)} %bitcast.42, bf16[3,5,50,1152]{3,2,1,0:T(8,128)(2,1)S(1)} %fusion.12, bf16[3,1,48,1152]{3,2,1,0:T(8,128)(2,1)S(1)} %collective-permute-done.3, bf16[3,1,48,1152]{3,2,1,0:T(8,128)(2,1)S(1)} %collective-permute-done.2, ...), kind=kLoop, calls=%fused_computation.24 | loop fusion | flops 14432256 | bytes 8667648 | tf_op jit(solution)/shard_map/convert_element_type | solution.py:90
  39.8 0.0 copy-start.9
  39.8 0.0 copy-start.11
  39.8 1.7 multiply_reduce_fusion
  41.6 1.3 copy-done.12
  42.8 1.7 convolution_convert_fusion
  44.5 0.0 copy-start.6
  44.5 4.0 %reshape.193 = bf16[27,16,16,72]{3,2,1,0:T(8,128)(2,1)} reshape(bf16[432,1152]{1,0:T(8,128)(2,1)S(1)} %convolution_convert_fusion) | data formatting | bytes 1990656 | tf_op jit(solution)/shard_map/reshape | solution.py:137
  48.6 0.0 collective-permute-done.4
  48.6 0.0 collective-permute-done.5
  48.6 0.0 collective-permute-done.6
  48.6 58.4 %collective-permute-done.7 = bf16[3,3,2,8,2304]{4,3,2,1,0:T(8,128)(2,1)} collective-permute-done((bf16[3,3,2,8,2304]{4,3,2,1,0:T(8,128)(2,1)}, bf16[3,3,2,8,2304]{4,3,2,1,0:T(8,128)(2,1)}, u32[]{:S(2)}, u32[]{:S(2)}) %collective-permute-start.7) | collective-permute-done | bytes 663584 | tf_op jit(solution)/shard_map/ppermute | solution.py:33
  106.9 1.7 select_bitcast_fusion.3
  108.7 0.2 maximum_bitcast_fusion
  108.9 0.2 pad_maximum_fusion
  109.2 8.9 %gather_fusion = bf16[216,8,2304]{2,1,0:T(8,128)(2,1)} fusion(bf16[72,8,2304]{2,1,0:T(8,128)(2,1)S(1)} %bitcast.38, s32[1024]{0:T(1024)S(1)} %pad_clamp_fusion), kind=kCustom, calls=%fused_computation | custom fusion | bytes 15926112 | tf_op jit(solution)/shard_map/jit(_take)/gather | solution.py:131
  118.1 4.1 %bitcast_select_fusion = bf16[27,64,2304]{2,1,0:T(8,128)(2,1)S(1)} fusion(pred[27,64]{1,0:T(8,128)(4,1)S(1)} %copy.32, bf16[27,64,2304]{2,1,0:T(8,128)(2,1)} %bitcast.39), kind=kLoop, calls=%fused_computation.2 | loop fusion | flops 3981312 | bytes 15926976 | tf_op jit(solution)/shard_map/jit(_take)/select_n | solution.py:131
  122.2 3.6 %fusion.32 = (bf16[27,64,1152]{2,1,0:T(8,128)(2,1)}, bf16[27,64,1152]{2,1,0:T(8,128)(2,1)}) fusion(bf16[27,64,2304]{2,1,0:T(8,128)(2,1)S(1)} %bitcast_select_fusion), kind=kLoop, calls=%fused_computation.93 | loop fusion | bytes 15925248 | tf_op jit(solution)/shard_map/slice | solution.py:134
  125.7 15.0 %reshape.194 = bf16[27,64,16,72]{3,2,1,0:T(8,128)(2,1)} reshape(bf16[27,64,1152]{2,1,0:T(8,128)(2,1)} %get-tuple-element.17) | data formatting | bytes 7962624 | tf_op jit(solution)/shard_map/reshape | solution.py:133
  140.7 15.1 %reshape.191 = bf16[27,64,16,72]{3,2,1,0:T(8,128)(2,1)} reshape(bf16[27,64,1152]{2,1,0:T(8,128)(2,1)} %get-tuple-element.16) | data formatting | bytes 7962624 | tf_op jit(solution)/shard_map/reshape | solution.py:134
  155.8 6.1 %fusion.3 = f32[27,16,16,64]{3,2,1,0:T(8,128)S(1)} fusion(bf16[27,64,16,72]{3,2,1,0:T(8,128)(2,1)} %reshape.194, bf16[27,16,16,72]{3,2,1,0:T(8,128)(2,1)S(1)} %copy-done.2), kind=kOutput, calls=%fused_computation.5 | convolution fusion | flops 63700992 | bytes 6746112 | tf_op jit(solution)/shard_map/nthd,nkhd->nhtk/dot_general | solution.py:139
  161.9 3.0 %fusion.35 = (f32[27,16,16]{2,1,0:T(8,128)S(1)}, f32[27,16,16,64]{3,2,1,0:T(8,128)}) fusion(f32[27,16,16,64]{3,2,1,0:T(8,128)S(1)} %fusion.3, pred[27,64]{1,0:T(8,128)(4,1)S(1)} %copy.34), kind=kOutput, calls=%fused_computation.96 | output fusion | flops 2654271 | bytes 3568320 | tf_op jit(solution)/shard_map/sub | solution.py:147
  164.9 1.3 copy-done.3
  166.2 5.7 %convert_bitcast_fusion = bf16[27,16,16,72]{3,1,2,0:T(8,128)(2,1)S(1)} fusion(f32[27,16,16,64]{3,2,1,0:T(8,128)} %get-tuple-element.38, f32[27,16,16]{2,1,0:T(8,128)S(1)} %get-tuple-element.37, bf16[27,64,16,72]{3,2,1,0:T(8,128)(2,1)S(1)} %copy-done.3), kind=kOutput, calls=%fused_computation.29 | convolution fusion | flops 65083392 | bytes 6773760 | tf_op jit(solution)/shard_map/nhtk,nkhd->nthd/dot_general | solution.py:149
  171.8 0.5 copy.38
  172.3 2.8 %reshape.195 = bf16[432,1152]{1,0:T(8,128)(2,1)} reshape(bf16[27,16,16,72]{3,2,1,0:T(8,128)(2,1)S(1)} %copy.38) | data formatting | bytes 1990656 | tf_op jit(solution)/shard_map/reshape | solution.py:152
  175.1 5.3 %fusion.6 = bf16[432,1152]{1,0:T(8,128)(2,1)} fusion(f32[432,1152]{1,0:T(8,128)} %copy-done.12, bf16[432,1152]{1,0:T(8,128)(2,1)} %reshape.195, bf16[1152,1152]{1,0:T(8,128)(2,1)} %param.21), kind=kOutput, calls=%fused_computation.15 | convolution fusion | flops 1147613184 | bytes 6635520 | tf_op jit(solution)/shard_map/dot_general | solution.py:153
  (25 shorter events, 0.1 us)
Async XLA Ops:
  0.0 39.8 %copy-start = (bf16[1152,1152]{1,0:T(8,128)(2,1)S(1)}, bf16[1152,1152]{1,0:T(8,128)(2,1)}, u32[]{:S(2)}) copy-start(bf16[1152,1152]{1,0:T(8,128)(2,1)} %param.18) | copy-start | bytes 7962628
  0.0 48.6 %collective-permute-start.4 = (bf16[3,3,2,8,2304]{4,3,2,1,0:T(8,128)(2,1)}, bf16[3,3,2,8,2304]{4,3,2,1,0:T(8,128)(2,1)}, u32[]{:S(2)}, u32[]{:S(2)}) collective-permute-start(bf16[3,3,2,8,2304]{4,3,2,1,0:T(8,128)(2,1)} %param.14), channel_id=1, source_target_pairs={{0,4},{4,8},{8,12},{12,16},{16,20},{20,24},{24,28},{28,32},{32,36}... | collective-permute-start | bytes 1990664 | tf_op jit(solution)/shard_map/ppermute | solution.py:33
  3.1 45.5 %collective-permute-start.5 = (bf16[3,3,2,8,2304]{4,3,2,1,0:T(8,128)(2,1)}, bf16[3,3,2,8,2304]{4,3,2,1,0:T(8,128)(2,1)}, u32[]{:S(2)}, u32[]{:S(2)}) collective-permute-start(bf16[3,3,2,8,2304]{4,3,2,1,0:T(8,128)(2,1)} %param.14), channel_id=1, source_target_pairs={{4,0},{8,4},{12,8},{16,12},{20,16},{24,20},{28,24},{32,28},{36,32}... | collective-permute-start | bytes 1990664 | tf_op jit(solution)/shard_map/ppermute | solution.py:33
  5.6 43.0 %collective-permute-start.6 = (bf16[3,3,2,8,2304]{4,3,2,1,0:T(8,128)(2,1)}, bf16[3,3,2,8,2304]{4,3,2,1,0:T(8,128)(2,1)}, u32[]{:S(2)}, u32[]{:S(2)}) collective-permute-start(bf16[3,3,2,8,2304]{4,3,2,1,0:T(8,128)(2,1)} %param.14), channel_id=1, source_target_pairs={{0,8},{4,12},{8,16},{12,20},{16,24},{20,28},{24,32},{28,36},{32,40... | collective-permute-start | bytes 1990664 | tf_op jit(solution)/shard_map/ppermute | solution.py:33
  11.6 8.9 %collective-permute-start = (s32[3,1,48]{2,1,0:T(1,128)S(1)}, s32[3,1,48]{2,1,0:T(1,128)S(1)}, u32[]{:S(2)}, u32[]{:S(2)}) collective-permute-start(s32[3,1,48]{2,1,0:T(1,128)S(1)} %get-tuple-element.33), channel_id=1, source_target_pairs={{0,1},{1,2},{2,3},{4,5},{5,6},{6,7},{8,9},{9,10},{10,11},{12,13},{... | collective-permute-start | bytes 1736 | tf_op jit(solution)/shard_map/ppermute | solution.py:21
  12.9 7.7 %collective-permute-start.1 = (s32[3,1,48]{2,1,0:T(1,128)S(1)}, s32[3,1,48]{2,1,0:T(1,128)S(1)}, u32[]{:S(2)}, u32[]{:S(2)}) collective-permute-start(s32[3,1,48]{2,1,0:T(1,128)S(1)} %get-tuple-element.34), channel_id=1, source_target_pairs={{1,0},{2,1},{3,2},{5,4},{6,5},{7,6},{9,8},{10,9},{11,10},{13,12},{... | collective-permute-start | bytes 1736 | tf_op jit(solution)/shard_map/ppermute | solution.py:23
  24.1 9.1 %copy-start.8 = (s32[216,1]{0,1:T(1,128)S(1)}, s32[216,1]{0,1:T(1,128)}, u32[]{:S(2)}) copy-start(s32[216,1]{0,1:T(1,128)} %reshape.190) | copy-start | bytes 2596
  24.1 9.3 %copy-start.7 = (bf16[9,1152]{1,0:T(8,128)(2,1)S(1)}, bf16[9,1152]{1,0:T(8,128)(2,1)}, u32[]{:S(2)}) copy-start(bf16[9,1152]{1,0:T(8,128)(2,1)} %param.17) | copy-start | bytes 62212
  25.8 1.0 copy-start.4
  27.6 6.0 %collective-permute-start.2 = (bf16[3,1,48,1152]{3,2,1,0:T(8,128)(2,1)}, bf16[3,1,48,1152]{3,2,1,0:T(8,128)(2,1)S(1)}, u32[]{:S(2)}, u32[]{:S(2)}) collective-permute-start(bf16[3,1,48,1152]{3,2,1,0:T(8,128)(2,1)} %get-tuple-element.18), channel_id=1, source_target_pairs={{0,1},{1,2},{2,3},{4,5},{5,6},{6,7},{8,9},{9,10},{10,11},{12,13},{... | collective-permute-start | bytes 995336 | tf_op jit(solution)/shard_map/ppermute | solution.py:21
  28.9 6.9 %collective-permute-start.3 = (bf16[3,1,48,1152]{3,2,1,0:T(8,128)(2,1)}, bf16[3,1,48,1152]{3,2,1,0:T(8,128)(2,1)S(1)}, u32[]{:S(2)}, u32[]{:S(2)}) collective-permute-start(bf16[3,1,48,1152]{3,2,1,0:T(8,128)(2,1)} %get-tuple-element.19), channel_id=1, source_target_pairs={{1,0},{2,1},{3,2},{5,4},{6,5},{7,6},{9,8},{10,9},{11,10},{13,12},{... | collective-permute-start | bytes 995336 | tf_op jit(solution)/shard_map/ppermute | solution.py:23
  33.4 4.2 %copy-start.5 = (bf16[432,1152]{1,0:T(8,128)(2,1)S(1)}, bf16[432,1152]{1,0:T(8,128)(2,1)}, u32[]{:S(2)}) copy-start(bf16[432,1152]{1,0:T(8,128)(2,1)} %copy-done.4) | copy-start | bytes 2985988
  33.6 73.3 %collective-permute-start.7 = (bf16[3,3,2,8,2304]{4,3,2,1,0:T(8,128)(2,1)}, bf16[3,3,2,8,2304]{4,3,2,1,0:T(8,128)(2,1)}, u32[]{:S(2)}, u32[]{:S(2)}) collective-permute-start(bf16[3,3,2,8,2304]{4,3,2,1,0:T(8,128)(2,1)} %param.14), channel_id=1, source_target_pairs={{0,12},{4,16},{8,20},{12,24},{16,28},{20,32},{24,36},{28,40},{32,4... | collective-permute-start | bytes 1990664 | tf_op jit(solution)/shard_map/ppermute | solution.py:33
  37.7 2.1 %copy-start.10 = (bf16[3,3,48,1152]{3,2,1,0:T(8,128)(2,1)S(1)}, bf16[3,3,48,1152]{3,2,1,0:T(8,128)(2,1)}, u32[]{:S(2)}) copy-start(bf16[3,3,48,1152]{3,2,1,0:T(8,128)(2,1)} %param.11) | copy-start | bytes 2985988
  39.8 3.0 %copy-start.9 = (bf16[1152,1152]{1,0:T(8,128)(2,1)S(1)}, bf16[1152,1152]{1,0:T(8,128)(2,1)}, u32[]{:S(2)}) copy-start(bf16[1152,1152]{1,0:T(8,128)(2,1)} %param.20) | copy-start | bytes 7962628
  39.8 3.0 %copy-start.11 = (f32[1152]{0:T(1024)S(1)}, f32[1152]{0:T(1024)}, u32[]{:S(2)}) copy-start(f32[1152]{0:T(1024)} %param.19) | copy-start | bytes 13828
  41.5 1.3 copy-start.12
  44.5 62.4 %copy-start.6 = (bf16[3,3,2,8,2304]{4,3,2,1,0:T(8,128)(2,1)S(1)}, bf16[3,3,2,8,2304]{4,3,2,1,0:T(8,128)(2,1)}, u32[]{:S(2)}) copy-start(bf16[3,3,2,8,2304]{4,3,2,1,0:T(8,128)(2,1)} %param.14) | copy-start | bytes 1990660
  140.7 15.1 %copy-start.2 = (bf16[27,16,16,72]{3,2,1,0:T(8,128)(2,1)S(1)}, bf16[27,16,16,72]{3,2,1,0:T(8,128)(2,1)}, u32[]{:S(2)}) copy-start(bf16[27,16,16,72]{3,2,1,0:T(8,128)(2,1)} %reshape.193) | copy-start | bytes 2985988
  161.9 4.3 %copy-start.3 = (bf16[27,64,16,72]{3,2,1,0:T(8,128)(2,1)S(1)}, bf16[27,64,16,72]{3,2,1,0:T(8,128)(2,1)}, u32[]{:S(2)}) copy-start(bf16[27,64,16,72]{3,2,1,0:T(8,128)(2,1)} %reshape.191) | copy-start | bytes 11943940
  175.1 5.3 %copy-start.1 = (bf16[1152,1152]{1,0:T(8,128)(2,1)S(1)}, bf16[1152,1152]{1,0:T(8,128)(2,1)}, u32[]{:S(2)}) copy-start(bf16[1152,1152]{1,0:T(8,128)(2,1)} %param.18) | copy-start | bytes 7962628
where the time goes:
time: 182 us; the launch traced here: 180 us
  local copies, waits for them, and re-layouts  59 us (32%)
  waiting for transfers between devices  58.4 us (32%)
  starting transfers between devices  23.9 us (13%)
  matrix products  22.1 us (12%)
  other arithmetic  16.7 us (9%)
    ppermute x4, waiting for transfers between devices, passed_along(): return lax.ppermute(block, axis, route)  58.4 us
    reshape x1, local copies, waits for them, and re-layouts, body(): slot_tiles[..., d_model:]  15.1 us
    reshape x1, local copies, waits for them, and re-layouts, body(): slot_tiles[..., :d_model]  15 us
    ppermute x4, starting transfers between devices, passed_along(): return lax.ppermute(block, axis, route)  13 us
    gather x1, local copies, waits for them, and re-layouts, body(): slot_tiles = jnp.take(tile_table, tile_id.reshape(-1), axis=0)  8.92 us
    ppermute x2, starting transfers between devices, with_halo(): lax.ppermute(head, axis, [((i + 1) % count, i) for i in range(ends)])  8.34 us
    dot_general x1, matrix products, body(): jnp.einsum('nthd,nkhd->nhtk', query_tiles, slot_keys, preferred_element_t...  6.07 us
    dot_general x1, matrix products, body(): jnp.einsum('nhtk,nkhd->nthd', weights_bf, slot_values, preferred_element_...  5.65 us
  transfers between devices with their start and end apart: 8, of which 1 were waited for; matrix products, arithmetic and copies ran while one was open for 12% of the time, Pallas kernels for 0%

commit v1 on v0

v1 whole, which is shorter than its diff:
```python
import functools

import jax
import jax.numpy as jnp
from jax import lax
from jax.experimental import pallas as pl
from jax.experimental.pallas import tpu as pltpu
from jax.sharding import PartitionSpec as P

HEADS = 16
HEAD = 72
CLASSES = 8
QT = 16
TW = 8
LANES = 128
WIN = 256
KEYS = 128
NEG = -1e30


def dot(a, b):
    return jnp.dot(a, b, preferred_element_type=jnp.float32)


def pre_kernel(
    views,
    rows,
    cols,
    up_ref,
    own_ref,
    down_ref,
    cw_ref,
    dw_ref,
    gain_ref,
    tok_hbm,
    zw_hbm,
    qw_hbm,
    hidden_ref,
    query_ref,
    cls_buf,
    oh_buf,
    dep_buf,
    tok_buf,
    zw_buf,
    qw_buf,
    sems,
):
    copies = [
        pltpu.make_async_copy(zw_hbm, zw_buf, sems.at[0]),
        pltpu.make_async_copy(tok_hbm, tok_buf, sems.at[1]),
        pltpu.make_async_copy(qw_hbm, qw_buf, sems.at[2]),
    ]
    for copy in copies:
        copy.start()
    d_model = zw_buf.shape[0]
    ext = rows + 4
    feat_rows = rows + 2
    here = lax.axis_index("row")
    first = here == 0
    last = here == lax.axis_size("row") - 1

    cls_buf[...] = jnp.full(cls_buf.shape, -1, jnp.int32)
    for v in range(views):
        for r in range(2):
            row = up_ref[v, pl.ds(rows - 2 + r, 1), :]
            cls_buf[pl.ds(v * ext + r, 1), pl.ds(0, cols)] = jnp.where(first, -1, row)
            row = down_ref[v, pl.ds(r, 1), :]
            cls_buf[pl.ds(v * ext + 2 + rows + r, 1), pl.ds(0, cols)] = jnp.where(last, -1, row)
        for r in range(rows):
            cls_buf[pl.ds(v * ext + 2 + r, 1), pl.ds(0, cols)] = own_ref[v, pl.ds(r, 1), :]
    cells = cls_buf[...]
    shifted = (pltpu.roll(cells, 1, axis=1), cells, pltpu.roll(cells, LANES - 1, axis=1))
    kind = lax.broadcasted_iota(jnp.int32, (CLASSES, LANES), 0)
    for v in range(views):
        for y in range(feat_rows):
            taps = []
            for a in range(3):
                for b in range(3):
                    at = v * ext + y + a
                    row = jnp.broadcast_to(shifted[b][at : at + 1, :], (CLASSES, LANES))
                    taps.append(jnp.where(row == kind, 1.0, 0.0).astype(jnp.float32))
            block = jnp.concatenate(taps, axis=0).T
            oh_buf[pl.ds((v * feat_rows + y) * cols, cols), :] = block[:cols, :].astype(jnp.bfloat16)

    column = lax.broadcasted_iota(jnp.int32, (cols, LANES), 0)

    def conv(chunk, carry):
        lanes = pl.ds(pl.multiple_of(chunk * LANES, LANES), LANES)
        weight = cw_ref[:, lanes]
        taps = dw_ref[:, lanes].astype(jnp.float32)
        for v in range(views):
            onehot = oh_buf[pl.ds(v * feat_rows * cols, feat_rows * cols), :]
            raw = dot(onehot, weight)
            feat = (raw / (1.0 + jnp.exp(-raw))).astype(jnp.bfloat16).astype(jnp.float32)
            line = []
            for y in range(feat_rows):
                part = feat[y * cols : (y + 1) * cols]
                if y == 0:
                    part = jnp.where(first, 0.0, part)
                if y == feat_rows - 1:
                    part = jnp.where(last, 0.0, part)
                line.append(part)
            for y in range(rows):
                sides = []
                for b in range(3):
                    total = line[y] * taps[b : b + 1]
                    for a in (1, 2):
                        total = total + line[y + a] * taps[3 * a + b : 3 * a + b + 1]
                    sides.append(total)
                left = jnp.where(column == 0, 0.0, pltpu.roll(sides[0], 1, axis=0))
                right = jnp.where(column == cols - 1, 0.0, pltpu.roll(sides[2], cols - 1, axis=0))
                out = (sides[1] + left + right).astype(jnp.bfloat16)
                dep_buf[pl.ds((v * rows + y) * cols, cols), lanes] = out
        return carry

    lax.fori_loop(0, d_model // LANES, conv, 0)
    copies[0].wait()
    copies[1].wait()
    hidden = tok_buf[...].astype(jnp.float32) + dot(dep_buf[...], zw_buf[...])
    hidden_ref[...] = hidden
    scale = lax.rsqrt(jnp.mean(hidden * hidden, axis=-1, keepdims=True) + 1e-06)
    normed = (hidden_ref[...] * scale * gain_ref[...]).astype(jnp.bfloat16)
    copies[2].wait()
    query_ref[...] = dot(normed, qw_buf[...]).astype(jnp.bfloat16)


def relay_kernel(per_half, loop_ref, own, other, msg, sems):
    half = lax.rem(lax.axis_index("camframe"), 2)
    for i in range(per_half):
        for side in range(2):
            view = (1 - half) * per_half + i
            cam = loop_ref[view, side]
            local = lax.rem(cam, per_half)
            mine = lax.div(cam, per_half) == half
            sem = sems.at[2 * i + side]

            @pl.when(mine)
            def _():
                pltpu.make_async_copy(own.at[local, :, 1 - side], msg.at[i, side], sem).start()

            @pl.when(jnp.logical_not(mine))
            def _():
                pltpu.make_async_copy(other.at[local, :, 1 - side], msg.at[i, side], sem).start()

    for i in range(per_half):
        for side in range(2):
            pltpu.make_async_copy(own.at[0, :, 0], msg.at[i, side], sems.at[2 * i + side]).wait()


def post_kernel(
    views,
    rows,
    cols,
    loop_ref,
    list_ref,
    hidden_ref,
    query_ref,
    own,
    other,
    prev,
    ow_hbm,
    out_ref,
    kv_buf,
    ow_buf,
    live_buf,
    up_buf,
    att_buf,
    ow_sem,
    kv_sems,
):
    position = lax.axis_index("camframe")
    frame = lax.div(position, 2)
    half = lax.rem(position, 2)
    d_model = ow_buf.shape[0]
    tokens = rows * cols
    for i in range(views):
        for side in range(2):
            cam = loop_ref[half * views + i, side]
            local = lax.rem(cam, views)
            mine = lax.div(cam, views) == half
            for r in range(rows):
                spot = kv_buf.at[i, pl.ds((side * rows + r) * TW, TW)]
                sem = kv_sems.at[(2 * i + side) * rows + r]

                @pl.when(mine)
                def _():
                    pltpu.make_async_copy(own.at[local, r, 1 - side], spot, sem).start()

                @pl.when(jnp.logical_not(mine))
                def _():
                    pltpu.make_async_copy(other.at[local, r, 1 - side], spot, sem).start()

    old = []
    for i in range(views):
        old.append(
            pltpu.make_async_copy(
                prev.at[i],
                kv_buf.at[i, pl.ds(2 * rows * TW, 2 * rows * TW)],
                kv_sems.at[2 * views * rows + i],
            )
        )
        old[-1].start()
    weight = pltpu.make_async_copy(ow_hbm, ow_buf, ow_sem)
    weight.start()
    pad = KEYS - 4 * rows * TW
    for i in range(views):
        kv_buf[i, pl.ds(KEYS - pad, pad), :] = jnp.zeros((pad, 2 * d_model), jnp.bfloat16)

    entry = lax.broadcasted_iota(jnp.int32, (cols // QT, KEYS), 1) // TW
    known = jnp.logical_or(entry < 2 * rows, frame > 0)
    for v in range(views):
        for r in range(rows):
            lists = list_ref[v, r]
            hit = jnp.zeros((cols // QT, KEYS), jnp.int32)
            for k in range(lists.shape[1]):
                hit = jnp.where(lists[:, k : k + 1] == entry, 1, hit)
            hit = jnp.where(known, hit, 0)
            for q in range(cols // QT):
                live_buf[v, pl.ds(r * cols + q * QT, QT), :] = jnp.broadcast_to(
                    hit[q : q + 1, :], (QT, KEYS)
                )

    for i in range(views):
        for side in range(2):
            for r in range(rows):
                spot = kv_buf.at[i, pl.ds((side * rows + r) * TW, TW)]
                sem = kv_sems.at[(2 * i + side) * rows + r]
                pltpu.make_async_copy(own.at[0, 0, 0], spot, sem).wait()
        old[i].wait()

    up_buf[...] = jnp.zeros_like(up_buf)
    score_scale = HEAD ** (-0.5)
    lane = lax.broadcasted_iota(jnp.int32, (KEYS, WIN), 1)

    def attend(pair, carry):
        base = pl.multiple_of(pair * LANES, LANES)
        start = pair * (2 * HEAD - LANES)
        heads = []
        for h in range(2):
            low = start + h * HEAD
            heads.append(jnp.logical_and(lane >= low, lane < low + HEAD))
        for v in range(views):
            query = query_ref[pl.ds(v * tokens, tokens), pl.ds(base, WIN)]
            key = kv_buf[v, :, pl.ds(base, WIN)]
            value = kv_buf[v, :, pl.ds(pl.multiple_of(base + d_model, LANES), WIN)]
            zero = jnp.zeros_like(key)
            keys = jnp.concatenate([jnp.where(m, key, zero) for m in heads], axis=0)
            values = jnp.concatenate([jnp.where(m, value, zero) for m in heads], axis=0)
            scores = lax.dot_general(
                query, keys, (((1,), (1,)), ((), ())), preferred_element_type=jnp.float32
            )
            live = live_buf[v] > 0
            probs = []
            for h in range(2):
                s = jnp.where(live, scores[:, h * KEYS : (h + 1) * KEYS] * score_scale, NEG)
                e = jnp.exp(s - jnp.max(s, axis=-1, keepdims=True))
                probs.append((e / jnp.sum(e, axis=-1, keepdims=True)).astype(jnp.bfloat16))
            got = dot(jnp.concatenate(probs, axis=1), values)
            att_buf[pl.ds(v * tokens, tokens), pl.ds(base, LANES)] = (
                got[:, :LANES] + up_buf[v]
            ).astype(jnp.bfloat16)
            up_buf[v] = got[:, LANES:]
        return carry

    lax.fori_loop(0, HEADS // 2, attend, 0)
    for v in range(views):
        att_buf[pl.ds(v * tokens, tokens), pl.ds(d_model - LANES, LANES)] = up_buf[v].astype(
            jnp.bfloat16
        )
    weight.wait()
    out_ref[...] = (hidden_ref[...] + dot(att_buf[...], ow_buf[...])).astype(jnp.bfloat16)


def body(
    tokens,
    classes,
    tile_lists,
    kv_cache,
    camera_loop,
    class_weight,
    depth_weight,
    zero_weight,
    norm_gain,
    query_weight,
    out_weight,
):
    views, rows, cols, d_model = tokens.shape
    count = views * rows * cols
    vmem = pl.BlockSpec(memory_space=pltpu.VMEM)
    smem = pl.BlockSpec(memory_space=pltpu.SMEM)
    hbm = pl.BlockSpec(memory_space=pl.ANY)
    params = pltpu.CompilerParams(vmem_limit_bytes=56 * 1024 * 1024)

    frames2 = lax.axis_size("camframe")
    ends = lax.axis_size("row") - 1
    other = lax.ppermute(kv_cache, "camframe", [(i, i ^ 1) for i in range(frames2)])
    up = lax.ppermute(classes, "row", [(i, i + 1) for i in range(ends)])
    down = lax.ppermute(classes, "row", [(i + 1, i) for i in range(ends)])

    hidden, queries = pl.pallas_call(
        functools.partial(pre_kernel, views, rows, cols),
        out_shape=(
            jax.ShapeDtypeStruct((count, d_model), jnp.float32),
            jax.ShapeDtypeStruct((count, d_model), jnp.bfloat16),
        ),
        in_specs=[vmem] * 6 + [hbm] * 3,
        out_specs=(vmem, vmem),
        scratch_shapes=[
            pltpu.VMEM((-(-views * (rows + 4) // 8) * 8, LANES), jnp.int32),
            pltpu.VMEM((views * (rows + 2) * cols, 9 * CLASSES), jnp.bfloat16),
            pltpu.VMEM((count, d_model), jnp.bfloat16),
            pltpu.VMEM((count, d_model), jnp.bfloat16),
            pltpu.VMEM((d_model, d_model), jnp.bfloat16),
            pltpu.VMEM((d_model, d_model), jnp.bfloat16),
            pltpu.SemaphoreType.DMA((3,)),
        ],
        compiler_params=params,
        name="pre",
    )(
        up,
        classes,
        down,
        class_weight,
        depth_weight,
        norm_gain.reshape(1, d_model),
        tokens.reshape(count, d_model),
        zero_weight,
        query_weight,
    )

    edge = kv_cache.shape[3]
    msg = pl.pallas_call(
        functools.partial(relay_kernel, views),
        out_shape=jax.ShapeDtypeStruct((views, 2, rows, edge, 2 * d_model), jnp.bfloat16),
        in_specs=[smem, hbm, hbm],
        out_specs=hbm,
        scratch_shapes=[pltpu.SemaphoreType.DMA((2 * views,))],
        compiler_params=params,
        name="relay",
    )(camera_loop, kv_cache, other)
    route = [(i, (i // 2 + 1) * 2 + 1 - i % 2) for i in range(frames2 - 2)]
    prev = lax.ppermute(msg, "camframe", route)

    result = pl.pallas_call(
        functools.partial(post_kernel, views, rows, cols),
        out_shape=jax.ShapeDtypeStruct((count, d_model), jnp.bfloat16),
        in_specs=[smem] + [vmem] * 3 + [hbm] * 4,
        out_specs=vmem,
        scratch_shapes=[
            pltpu.VMEM((views, KEYS, 2 * d_model), jnp.bfloat16),
            pltpu.VMEM((d_model, d_model), jnp.bfloat16),
            pltpu.VMEM((views, rows * cols, KEYS), jnp.int32),
            pltpu.VMEM((views, rows * cols, LANES), jnp.float32),
            pltpu.VMEM((count, d_model), jnp.bfloat16),
            pltpu.SemaphoreType.DMA,
            pltpu.SemaphoreType.DMA((2 * views * rows + views,)),
        ],
        compiler_params=params,
        name="post",
    )(
        camera_loop,
        tile_lists,
        hidden,
        queries,
        kv_cache,
        other,
        prev.reshape(views, 2 * rows * edge, 2 * d_model),
        out_weight,
    )
    return result.reshape(views, rows, cols, d_model)


def solution(mesh):
    return jax.shard_map(
        body,
        mesh=mesh,
        in_specs=(
            P("camframe", "row", None, None),
            P("camframe", "row", None),
            P("camframe", "row", None, None),
            P("camframe", "row", None, None, None),
            P(),
            P(),
            P(),
            P(),
            P(),
            P(),
            P(),
        ),
        out_specs=P("camframe", "row", None, None),
        check_vma=False,
    )
```

time: 182 us -> 98.6 us (0.54)
  the two profiles are of different devices: /device:TPU:101 before, /device:TPU:124 now
where the time goes in v1:
time: 98.6 us; the launch traced here: 98.3 us
  Pallas kernels  46.7 us (47%)
  waiting for transfers between devices  34.8 us (35%)
  starting transfers between devices  11.9 us (12%)
  local copies, waits for them, and re-layouts  4.92 us (5%)
    pallas_call x1, Pallas kernels, body(): pl.pallas_call(functools.partial(relay_kernel, views), out_shape=jax.Shap...  22 us
    ppermute x1, waiting for transfers between devices, body(): up = lax.ppermute(classes, 'row', [(i, i + 1) for i in range(ends)])  20.4 us
    pallas_call x1, Pallas kernels, body(): pl.pallas_call(functools.partial(post_kernel, views, rows, cols), out_sha...  14.8 us
    ppermute x1, waiting for transfers between devices, body(): lax.ppermute(kv_cache, 'camframe', [(i, i ^ 1) for i in range(frames2)])  14.3 us
    pallas_call x1, Pallas kernels, body(): pl.pallas_call(functools.partial(pre_kernel, views, rows, cols), out_shap...  9.86 us
    ppermute x1, starting transfers between devices, body(): prev = lax.ppermute(msg, 'camframe', route)  5.12 us
    ppermute x1, starting transfers between devices, body(): down = lax.ppermute(classes, 'row', [(i + 1, i) for i in range(ends)])  3.64 us
    unnamed x9, local copies, waits for them, and re-layouts  3.63 us
  transfers between devices with their start and end apart: 4, of which 2 were waited for; matrix products, arithmetic and copies ran while one was open for 3% of the time, Pallas kernels for 10%

profile of v1, /device:TPU:124, one launch (start us, length us, event | category | flops | bytes accessed | tf_op | source)
XLA Modules:
  0.0 98.3 jit_solution(9454892112554077992)
XLA Ops:
  0.0 1.2 %collective-permute-start.2 = (bf16[3,3,2,8,2304]{4,3,2,1,0:T(8,128)(2,1)}, bf16[3,3,2,8,2304]{4,3,2,1,0:T(8,128)(2,1)S(1)}, u32[]{:S(2)}, u32[]{:S(2)}) collective-permute-start(bf16[3,3,2,8,2304]{4,3,2,1,0:T(8,128)(2,1)} %own.3), channel_id=1, source_target_pairs={{0,4},{4,0},{8,12},{12,8},{16,20},{20,16},{24,28},{28,24},{32,36},... | collective-permute-start | bytes 1990664 | tf_op jit(solution)/shard_map/ppermute | solution.py:296
  1.2 1.3 %copy.13.loop_ref = s32[6,2]{1,0:T(8,128)} copy(s32[6,2]{0,1:T(2,128)} %param.15) | data formatting | bytes 96 | tf_op args[4]
  2.5 14.3 %collective-permute-done.2.other = bf16[3,3,2,8,2304]{4,3,2,1,0:T(8,128)(2,1)S(1)} collective-permute-done((bf16[3,3,2,8,2304]{4,3,2,1,0:T(8,128)(2,1)}, bf16[3,3,2,8,2304]{4,3,2,1,0:T(8,128)(2,1)S(1)}, u32[]{:S(2)}, u32[]{:S(2)}) %collective-permute-start.2) | collective-permute-done | bytes 663584 | tf_op jit(solution)/shard_map/ppermute | solution.py:296
  16.9 0.0 copy-start
  16.9 0.8 copy-done
  17.7 22.0 %relay.1 = bf16[3,2,3,8,2304]{4,3,2,1,0:T(8,128)(2,1)} custom-call(s32[6,2]{1,0:T(8,128)} %copy.13.loop_ref, bf16[3,3,2,8,2304]{4,3,2,1,0:T(8,128)(2,1)} %own.3, bf16[3,3,2,8,2304]{4,3,2,1,0:T(8,128)(2,1)} %copy-done), custom_call_target="tpu_custom_call" | custom-call | tf_op jit(solution)/shard_map/relay/pallas_call | solution.py:332
  39.7 5.1 %collective-permute-start.3 = (bf16[3,2,3,8,2304]{4,3,2,1,0:T(8,128)(2,1)}, bf16[3,2,3,8,2304]{4,3,2,1,0:T(8,128)(2,1)S(1)}, u32[]{:S(2)}, u32[]{:S(2)}) collective-permute-start(bf16[3,2,3,8,2304]{4,3,2,1,0:T(8,128)(2,1)} %relay.1), channel_id=1, source_target_pairs={{0,12},{4,8},{8,20},{12,16},{16,28},{20,24},{24,36},{28,32},{32,44... | collective-permute-start | bytes 1990664 | tf_op jit(solution)/shard_map/ppermute | solution.py:342
  44.9 1.9 %collective-permute-start = (s32[3,3,48]{2,1,0:T(4,128)}, s32[3,3,48]{2,1,0:T(4,128)S(1)}, u32[]{:S(2)}, u32[]{:S(2)}) collective-permute-start(s32[3,3,48]{2,1,0:T(4,128)} %own_ref.1), channel_id=1, source_target_pairs={{0,1},{1,2},{2,3},{4,5},{5,6},{6,7},{8,9},{9,10},{10,11},{12,13},{... | collective-permute-start | bytes 5192 | tf_op jit(solution)/shard_map/ppermute | solution.py:297
  46.8 3.6 %collective-permute-start.1 = (s32[3,3,48]{2,1,0:T(4,128)}, s32[3,3,48]{2,1,0:T(4,128)S(1)}, u32[]{:S(2)}, u32[]{:S(2)}) collective-permute-start(s32[3,3,48]{2,1,0:T(4,128)} %own_ref.1), channel_id=1, source_target_pairs={{1,0},{2,1},{3,2},{5,4},{6,5},{7,6},{9,8},{10,9},{11,10},{13,12},{... | collective-permute-start | bytes 5192 | tf_op jit(solution)/shard_map/ppermute | solution.py:298
  50.4 1.3 %reshape.12.gain_ref = f32[1,1152]{1,0:T(1,128)} reshape(f32[1152]{0:T(1024)} %param.19) | data formatting | bytes 9216 | tf_op jit(solution)/shard_map/reshape | solution.py:325
  51.7 20.4 %collective-permute-done.up_ref = s32[3,3,48]{2,1,0:T(4,128)S(1)} collective-permute-done((s32[3,3,48]{2,1,0:T(4,128)}, s32[3,3,48]{2,1,0:T(4,128)S(1)}, u32[]{:S(2)}, u32[]{:S(2)}) %collective-permute-start) | collective-permute-done | bytes 1760 | tf_op jit(solution)/shard_map/ppermute | solution.py:297
  72.2 0.0 copy-start.2
  72.2 0.0 collective-permute-done.1.down_ref
  72.2 0.0 copy-start.3
  72.2 0.6 copy-done.2
  72.8 0.0 copy-done.3
  72.8 9.9 %pre.1 = (f32[432,1152]{1,0:T(8,128)}, bf16[432,1152]{1,0:T(8,128)(2,1)}) custom-call(s32[3,3,48]{2,1,0:T(4,128)} %copy-done.2, s32[3,3,48]{2,1,0:T(4,128)} %own_ref.1, s32[3,3,48]{2,1,0:T(4,128)} %copy-done.3, bf16[72,1152]{1,0:T(8,128)(2,1)} %cw_ref.1, bf16[9,1152]{1,0:T(8,128)(2,1)} %dw_ref.1, f32[1,1152]{1,0:T(1,128)} %reshape.12.gain_ref, ...), custom_call_target="tpu_custom_call" | custom-call | tf_op jit(solution)/shard_map/pre/pallas_call | solution.py:300
  82.6 0.0 collective-permute-done.3
  82.6 0.0 copy-start.1
  82.7 0.8 copy-done.1
  83.5 14.8 %post.1 = bf16[432,1152]{1,0:T(8,128)(2,1)} custom-call(s32[6,2]{1,0:T(8,128)} %copy.13.loop_ref, s32[3,3,3,8]{3,2,1,0:T(4,128)} %list_ref.1, f32[432,1152]{1,0:T(8,128)} %get-tuple-element.7.hidden_ref, bf16[432,1152]{1,0:T(8,128)(2,1)} %get-tuple-element.8.query_ref, bf16[3,3,2,8,2304]{4,3,2,1,0:T(8,128)(2,1)} %own.3, bf16[3,3,2,8,2304]{4,3,2,1,0:T(8,128)(2,1)} %copy-done, ...), custom_call_target="tpu_custom_call" | custom-call | tf_op jit(solution)/shard_map/post/pallas_call | solution.py:344
Async XLA Ops:
  0.0 16.9 %collective-permute-start.2 = (bf16[3,3,2,8,2304]{4,3,2,1,0:T(8,128)(2,1)}, bf16[3,3,2,8,2304]{4,3,2,1,0:T(8,128)(2,1)S(1)}, u32[]{:S(2)}, u32[]{:S(2)}) collective-permute-start(bf16[3,3,2,8,2304]{4,3,2,1,0:T(8,128)(2,1)} %own.3), channel_id=1, source_target_pairs={{0,4},{4,0},{8,12},{12,8},{16,20},{20,16},{24,28},{28,24},{32,36},... | collective-permute-start | bytes 1990664 | tf_op jit(solution)/shard_map/ppermute | solution.py:296
  16.9 0.8 copy-start
  39.7 42.9 %collective-permute-start.3 = (bf16[3,2,3,8,2304]{4,3,2,1,0:T(8,128)(2,1)}, bf16[3,2,3,8,2304]{4,3,2,1,0:T(8,128)(2,1)S(1)}, u32[]{:S(2)}, u32[]{:S(2)}) collective-permute-start(bf16[3,2,3,8,2304]{4,3,2,1,0:T(8,128)(2,1)} %relay.1), channel_id=1, source_target_pairs={{0,12},{4,8},{8,20},{12,16},{16,28},{20,24},{24,36},{28,32},{32,44... | collective-permute-start | bytes 1990664 | tf_op jit(solution)/shard_map/ppermute | solution.py:342
  44.9 27.3 %collective-permute-start = (s32[3,3,48]{2,1,0:T(4,128)}, s32[3,3,48]{2,1,0:T(4,128)S(1)}, u32[]{:S(2)}, u32[]{:S(2)}) collective-permute-start(s32[3,3,48]{2,1,0:T(4,128)} %own_ref.1), channel_id=1, source_target_pairs={{0,1},{1,2},{2,3},{4,5},{5,6},{6,7},{8,9},{9,10},{10,11},{12,13},{... | collective-permute-start | bytes 5192 | tf_op jit(solution)/shard_map/ppermute | solution.py:297
  46.8 25.4 %collective-permute-start.1 = (s32[3,3,48]{2,1,0:T(4,128)}, s32[3,3,48]{2,1,0:T(4,128)S(1)}, u32[]{:S(2)}, u32[]{:S(2)}) collective-permute-start(s32[3,3,48]{2,1,0:T(4,128)} %own_ref.1), channel_id=1, source_target_pairs={{1,0},{2,1},{3,2},{5,4},{6,5},{7,6},{9,8},{10,9},{11,10},{13,12},{... | collective-permute-start | bytes 5192 | tf_op jit(solution)/shard_map/ppermute | solution.py:298
  72.2 0.6 copy-start.2
  72.2 0.6 copy-start.3
  82.6 0.8 copy-start.1
